TPU v7x, 256 devices: a whole 4x4x8 slice. The times are simulated.
256 devices in a mesh: ctxa: 32 (over x, z), ctxb: 8 (over y, core).
Axes of the slice: x: 4, y: 4, z: 8, core: 2. Of those that a mesh axis runs over, the one named last changes fastest.
Arguments:
- tokens: bfloat16 [32768, 1024], P(('ctxa', 'ctxb')), may hold values from -80 to 80
- w_query: bfloat16 [1024, 512], replicated, may hold values from -0.1875 to 0.1875
- w_key: bfloat16 [1024, 512], replicated, may hold values from -0.1875 to 0.1875
- w_value: bfloat16 [1024, 512], replicated, may hold values from -0.1875 to 0.1875
- w_slot: bfloat16 [8, 64, 128], replicated, may hold values from -3 to 3
- w_out: bfloat16 [512, 1024], replicated, may hold values from -1 to 1
Outputs:
- mixed: bfloat16 [32768, 1024], P(('ctxa', 'ctxb'))
All inputs are finite; a program needn't handle non-finite values.
Results may differ from a plain program's by a relative error of at most 0.012.
The roundings to bfloat16 on the way count: a program that leaves them out, or rounds other values in their place, can miss the bound.
Values may be sent and summed in bfloat16 or wider, within the bound.
A program may use at most 192 MiB of HBM per device.

v0:
```python
import jax
import jax.numpy as jnp
from jax import lax
from jax.sharding import PartitionSpec as P

HEADS = 8
HEAD_DIM = 64
SLOTS = 128
WINDOW = 128


def padded_2(block, sides, width):
    for axis, dim in sides:
        count = lax.axis_size(axis)
        forward = [(i, i + 1) for i in range(count - 1)]
        backward = [(target, source) for source, target in forward]
        low = lax.ppermute(
            lax.slice_in_dim(block, block.shape[dim] - width, None, axis=dim), axis, forward
        )
        high = lax.ppermute(lax.slice_in_dim(block, 0, width, axis=dim), axis, backward)
        block = jnp.concatenate([low, block, high], axis=dim)
    return block


def layer_norm(values):
    center = values - jnp.mean(values, axis=-1, keepdims=True)
    spread = jnp.mean(center * center, axis=-1, keepdims=True)
    return center * lax.rsqrt(spread + 1e-05)


def finish_slots(total, sums):
    slot_keys = layer_norm(sums[..., :HEAD_DIM]).astype(jnp.bfloat16)
    slot_values = (sums[..., HEAD_DIM:] / total[..., None]).astype(jnp.bfloat16)
    return (slot_keys, slot_values)


def per_device(tokens, w_query, w_key, w_value, w_slot, w_out):
    rows = tokens.shape[0]
    width = HEADS * HEAD_DIM
    query = jnp.dot(tokens, w_query, preferred_element_type=jnp.float32).astype(jnp.bfloat16)
    key = jnp.dot(tokens, w_key, preferred_element_type=jnp.float32).astype(jnp.bfloat16)
    value = jnp.dot(tokens, w_value, preferred_element_type=jnp.float32).astype(jnp.bfloat16)
    key_heads = key.reshape(rows, HEADS, HEAD_DIM)
    logits = jnp.einsum("thd,hds->hts", key_heads, w_slot, preferred_element_type=jnp.float32)
    paired = jnp.concatenate([key_heads, value.reshape(rows, HEADS, HEAD_DIM)], axis=2).astype(
        jnp.float32
    )
    local_top = jnp.max(logits, axis=1)
    top = lax.pmax(local_top, ("ctxa", "ctxb"))
    weight = jnp.exp(logits - top[:, None, :])
    total = jnp.sum(weight, axis=1)
    sums = jnp.einsum("hts,thd->hsd", weight, paired, precision=lax.Precision.HIGHEST)
    total, sums = lax.psum((total, sums), ("ctxa", "ctxb"))
    slot_keys, slot_values = finish_slots(total, sums)
    near_keys = layer_norm(key_heads.astype(jnp.float32)).astype(jnp.bfloat16).reshape(rows, width)
    stacked = jnp.concatenate([near_keys, value], axis=1)
    padded = padded_2(stacked, ((("ctxa", "ctxb"), 0),), WINDOW)
    seq_len = rows * lax.axis_size(("ctxa", "ctxb"))
    offset = lax.axis_index(("ctxa", "ctxb")) * rows
    block = min(512, rows)
    span = block + 2 * WINDOW
    scale = 1.0 / HEAD_DIM**0.5
    groups = 2
    group_heads = HEADS // groups
    group_width = group_heads * HEAD_DIM
    grouped_keys = slot_keys.reshape(groups, group_heads, SLOTS, HEAD_DIM)
    grouped_values = slot_values.reshape(groups, group_heads, SLOTS, HEAD_DIM)
    blocks = rows // block

    def attend(item):
        index = item // groups
        group = item % groups
        start = index * block
        column = group * group_width
        query_block = lax.dynamic_slice_in_dim(query, column, group_width, 1).reshape(
            block, group_heads, HEAD_DIM
        )
        keys_block = lax.dynamic_slice_in_dim(padded, column, group_width, 1).reshape(
            span, group_heads, HEAD_DIM
        )
        values_block = lax.dynamic_slice_in_dim(padded, width + column, group_width, 1).reshape(
            span, group_heads, HEAD_DIM
        )
        group_slot_keys = lax.dynamic_index_in_dim(grouped_keys, group, 0, keepdims=False)
        group_slot_values = lax.dynamic_index_in_dim(grouped_values, group, 0, keepdims=False)
        query_pos = offset + start + jnp.arange(block, dtype=jnp.int32)
        key_pos = offset + start - WINDOW + jnp.arange(span, dtype=jnp.int32)
        valid = (
            (jnp.abs(key_pos[None, :] - query_pos[:, None]) <= WINDOW)
            & (key_pos[None, :] >= 0)
            & (key_pos[None, :] < seq_len)
        )
        near = (
            jnp.einsum("bhd,khd->hbk", query_block, keys_block, preferred_element_type=jnp.float32)
            * scale
        )
        near = jnp.where(valid[None], near, -1e30)
        far = (
            jnp.einsum(
                "bhd,hsd->hbs", query_block, group_slot_keys, preferred_element_type=jnp.float32
            )
            * scale
        )
        top_score = jnp.maximum(jnp.max(near, axis=-1), jnp.max(far, axis=-1))
        near_exp = jnp.exp(near - top_score[..., None])
        far_exp = jnp.exp(far - top_score[..., None])
        denom = jnp.sum(near_exp, axis=-1) + jnp.sum(far_exp, axis=-1)
        near_probs = (near_exp / denom[..., None]).astype(jnp.bfloat16)
        far_probs = (far_exp / denom[..., None]).astype(jnp.bfloat16)
        result = jnp.einsum(
            "hbk,khd->bhd", near_probs, values_block, preferred_element_type=jnp.float32
        )
        result = result + jnp.einsum(
            "hbs,hsd->bhd", far_probs, group_slot_values, preferred_element_type=jnp.float32
        )
        return result.reshape(block, group_width).astype(jnp.bfloat16)

    pieces = lax.map(attend, jnp.arange(blocks * groups, dtype=jnp.int32))
    attended = (
        pieces.reshape(blocks, groups, block, group_width)
        .transpose(0, 2, 1, 3)
        .reshape(rows, width)
    )
    return jnp.dot(attended, w_out, preferred_element_type=jnp.float32).astype(jnp.bfloat16)


def solution(mesh):
    in_specs = (P(("ctxa", "ctxb"), None), P(), P(), P(), P(), P())
    out_specs = P(("ctxa", "ctxb"), None)
    return jax.shard_map(
        per_device, mesh=mesh, in_specs=in_specs, out_specs=out_specs, check_vma=False
    )
```

profile of v0, /device:TPU:2, one launch (start us, length us, event | category | flops | bytes accessed | tf_op | source)
XLA Modules:
  0.0 378.1 jit_solution(4458475252980913308)
XLA Ops:
  6.5 1.8 convolution_convert_fusion.3
  8.5 0.3 convolution_convert_fusion.2
  9.3 0.7 pad_maximum_fusion.1
  10.0 1.9 collective-permute-start
  11.9 9.6 %collective-permute-start.1 = (bf16[128,1024]{1,0:T(8,128)(2,1)}, bf16[128,1024]{1,0:T(8,128)(2,1)}, u32[]{:S(2)}, u32[]{:S(2)}) collective-permute-start(bf16[128,1024]{1,0:T(8,128)(2,1)} %pad_maximum_fusion.1), channel_id=1, source_target_pairs={{1,0},{2,1},{3,2},{4,3},{5,4},{6,5},{7,6},{8,7},{9,8},{10,9},{11,1... | collective-permute-start | bytes 786440 | tf_op jit(solution)/shard_map/ppermute | solution.py:20
  21.7 0.9 copy.21
  22.6 0.3 fusion.27
  22.8 72.5 %pmax.7 = f32[8,128]{1,0:T(8,128)S(1)} all-reduce(f32[8,128]{1,0:T(8,128)S(1)} %get-tuple-element.154), channel_id=1, replica_groups=mesh['ctxa'=32,'ctxb'=8] {'ctxa','ctxb'}, use_global_device_ids=true, to_apply=%region_3.0 | all-reduce | flops 1024 | bytes 8192 | tf_op jit(solution)/shard_map/pmax | solution.py:49
  95.3 0.2 copy.22
  95.5 2.5 fusion.17
  98.1 75.0 %psum.15 = f32[8,128]{1,0:T(8,128)S(1)} all-reduce(f32[8,128]{1,0:T(8,128)S(1)} %fusion.16), channel_id=1, replica_groups=mesh['ctxa'=32,'ctxb'=8] {'ctxa','ctxb'}, use_global_device_ids=true, to_apply=%region_8.0 | all-reduce | flops 1024 | bytes 8192 | tf_op jit(solution)/shard_map/psum | solution.py:53
  173.1 0.3 convolution_convert_fusion.1
  173.5 179.0 %all-reduce.2.cloned.1.call-done = f32[8,128,128]{2,1,0:T(8,128)} async-done(((f32[8,128,128]{2,1,0:T(8,128)}), f32[8,128,128]{2,1,0:T(8,128)}) %all-reduce.2.cloned.1.call-update) | async-done | bytes 524304 | tf_op jit(solution)/shard_map/psum | solution.py:53
  352.4 1.3 slice_reduce_fusion
  353.8 1.4 multiply_reduce_fusion
  355.2 0.6 fusion.15
  356.1 1.1 pad_maximum_fusion
  357.2 0.4 copy.24
  357.6 11.7 %while.12 = (s32[]{:T(128)}, bf16[2,128,256]{1,2,0:T(8,128)(2,1)}, s32[2]{0:T(128)S(1)}, bf16[384,1024]{0,1:T(8,128)(2,1)S(1)}, s32[]{:T(128)}, /*index=5*/bf16[...) while((s32[]{:T(128)}, bf16[2,128,256]{1,2,0:T(8,128)(2,1)}, ...), condition=%wide.region_14.15_spmd, body=%wide.region_9.14_spmd.sunk | while | flops 69452448 | bytes 5446203 | solution.py:118
  357.6 0.6 dynamic_slice.60
  361.2 0.4 fusion.63
  361.6 0.3 fusion.60
  362.0 0.3 fusion.64
  362.4 0.4 fusion.67
  362.8 0.6 constant_dynamic-update-slice_fusion.2
  363.5 0.6 dynamic_slice.60
  367.1 0.4 fusion.63
  367.5 0.3 fusion.60
  367.8 0.3 fusion.64
  368.3 0.4 fusion.67
  368.7 0.6 constant_dynamic-update-slice_fusion.2
  369.3 1.9 convolution_convert_fusion
  (56 shorter events, 2.2 us)
Async XLA Ops:
  6.5 362.8 %copy-start = (bf16[512,1024]{1,0:T(8,128)(2,1)S(1)}, bf16[512,1024]{1,0:T(8,128)(2,1)}, u32[]{:S(2)}) copy-start(bf16[512,1024]{1,0:T(8,128)(2,1)} %param.13) | copy-start | bytes 3145732
  6.5 1.9 copy-start.2
  6.5 1.9 copy-start.3
  6.5 345.9 %all-reduce.2.cloned.1.call-start = ((), (), s32[]{:S(2)}) async-start(), calls=%async_computation | async-start | bytes 1048576 | tf_op jit(solution)/shard_map/psum | solution.py:53
  9.2 13.3 %copy-start.5 = (bf16[8,64,128]{2,1,0:T(8,128)(2,1)S(1)}, bf16[8,64,128]{2,1,0:T(8,128)(2,1)}, u32[]{:S(2)}) copy-start(bf16[8,64,128]{2,1,0:T(8,128)(2,1)} %param.12) | copy-start | bytes 393220
  10.0 346.1 %collective-permute-start = (bf16[128,1024]{1,0:T(8,128)(2,1)}, bf16[128,1024]{1,0:T(8,128)(2,1)}, u32[]{:S(2)}, u32[]{:S(2)}) collective-permute-start(bf16[128,1024]{1,0:T(8,128)(2,1)} %pad_maximum_fusion.1), channel_id=1, source_target_pairs={{0,1},{1,2},{2,3},{3,4},{4,5},{5,6},{6,7},{7,8},{8,9},{9,10},{10,1... | collective-permute-start | bytes 786440 | tf_op jit(solution)/shard_map/ppermute | solution.py:17
  11.9 344.2 %collective-permute-start.1 = (bf16[128,1024]{1,0:T(8,128)(2,1)}, bf16[128,1024]{1,0:T(8,128)(2,1)}, u32[]{:S(2)}, u32[]{:S(2)}) collective-permute-start(bf16[128,1024]{1,0:T(8,128)(2,1)} %pad_maximum_fusion.1), channel_id=1, source_target_pairs={{1,0},{2,1},{3,2},{4,3},{5,4},{6,5},{7,6},{8,7},{9,8},{10,9},{11,1... | collective-permute-start | bytes 786440 | tf_op jit(solution)/shard_map/ppermute | solution.py:20
  95.5 77.7 %copy-start.4 = (bf16[1024,512]{1,0:T(8,128)(2,1)S(1)}, bf16[1024,512]{1,0:T(8,128)(2,1)}, u32[]{:S(2)}) copy-start(bf16[1024,512]{1,0:T(8,128)(2,1)} %param.9) | copy-start | bytes 3145732
  352.4 2.8 copy-start.1
Sparse Core Ops, SparseCore 0:
  98.2 254.2 all-reduce.1
where the time goes:
time: 379 us; the launch traced here: 378 us
  waiting for transfers between devices  179 us (47%)
  blocking collectives  147 us (39%)
  between operations  13.7 us (4%)
  starting transfers between devices  11.5 us (3%)
  matrix products  9.54 us (3%)
  other arithmetic  6.44 us (2%)
  loops' own time  5.47 us (1%)
  local copies, waits for them, and re-layouts  4.99 us (1%)
    psum x1, waiting for transfers between devices, per_device(): total, sums = lax.psum((total, sums), ('ctxa', 'ctxb'))  179 us
    psum x1, blocking collectives, per_device(): total, sums = lax.psum((total, sums), ('ctxa', 'ctxb'))  75 us
    pmax x1, blocking collectives, per_device(): top = lax.pmax(local_top, ('ctxa', 'ctxb'))  72.5 us
    ppermute x1, starting transfers between devices, padded_2(): lax.ppermute(lax.slice_in_dim(block, 0, width, axis=dim), axis, backward)  9.63 us
  transfers between devices with their start and end apart: 3, of which 1 were waited for; matrix products, arithmetic and copies ran while one was open for 2% of the time, Pallas kernels for 0%

commit v1 on v0

--- a/solution.py
+++ b/solution.py
@@ -50,7 +50,7 @@
     weight = jnp.exp(logits - top[:, None, :])
     total = jnp.sum(weight, axis=1)
     sums = jnp.einsum("hts,thd->hsd", weight, paired, precision=lax.Precision.HIGHEST)
-    total, sums = lax.psum((total, sums), ("ctxa", "ctxb"))
+    total, sums = lax.psum(lax.psum((total, sums), "ctxb"), "ctxa")
     slot_keys, slot_values = finish_slots(total, sums)
     near_keys = layer_norm(key_heads.astype(jnp.float32)).astype(jnp.bfloat16).reshape(rows, width)
     stacked = jnp.concatenate([near_keys, value], axis=1)

time: 379 us -> 332 us (0.88)
  waiting for transfers between devices: 179 us -> 127 us
  blocking collectives: 147 us -> 155 us
    psum x1 -> x2, waiting for transfers between devices: 179 us -> 127 us  [per_device(): total, sums = lax.psum(lax.psum((total, sums), 'ctxb'), 'ctxa')]
    pmax x1, blocking collectives: 72.5 us -> 78.7 us  [per_device(): top = lax.pmax(local_top, ('ctxa', 'ctxb'))]
    psum x1 -> x2, blocking collectives: 75 us -> 76.5 us  [per_device(): total, sums = lax.psum(lax.psum((total, sums), 'ctxb'), 'ctxa')]
  transfers between devices with their start and end apart: 3 -> 4, of which waited for: 1 -> 2; matrix products, arithmetic and copies ran while one was open for 2% -> 1% of each run, Pallas kernels for 0% -> 0%
where the time goes in v1:
time: 332 us; the launch traced here: 331 us
  blocking collectives  155 us (47%)
  waiting for transfers between devices  127 us (38%)
  between operations  13.7 us (4%)
  starting transfers between devices  9.96 us (3%)
  matrix products  8.48 us (3%)
  loops' own time  5.81 us (2%)
  other arithmetic  5.73 us (2%)
  local copies, waits for them, and re-layouts  4.49 us (1%)
    psum x2, waiting for transfers between devices, per_device(): total, sums = lax.psum(lax.psum((total, sums), 'ctxb'), 'ctxa')  127 us
    pmax x1, blocking collectives, per_device(): top = lax.pmax(local_top, ('ctxa', 'ctxb'))  78.7 us
    psum x2, blocking collectives, per_device(): total, sums = lax.psum(lax.psum((total, sums), 'ctxb'), 'ctxa')  76.5 us
    ppermute x1, starting transfers between devices, padded_2(): lax.ppermute(lax.slice_in_dim(block, 0, width, axis=dim), axis, backward)  7.86 us
  transfers between devices with their start and end apart: 4, of which 2 were waited for; matrix products, arithmetic and copies ran while one was open for 1% of the time, Pallas kernels for 0%

profile of v1, /device:TPU:2, one launch (start us, length us, event | category | flops | bytes accessed | tf_op | source)
XLA Modules:
  0.0 330.5 jit_solution(11545820218254728413)
XLA Ops:
  6.5 1.7 convolution_convert_fusion.3
  8.4 0.2 copy.21
  8.6 0.3 fusion.27
  8.9 78.7 %pmax.7 = f32[8,128]{1,0:T(8,128)S(1)} all-reduce(f32[8,128]{1,0:T(8,128)S(1)} %get-tuple-element.154), channel_id=1, replica_groups=mesh['ctxa'=32,'ctxb'=8] {'ctxa','ctxb'}, use_global_device_ids=true, to_apply=%region_3.0 | all-reduce | flops 1024 | bytes 8192 | tf_op jit(solution)/shard_map/pmax | solution.py:49
  87.6 0.3 convolution_convert_fusion.2
  88.2 1.5 fusion.17
  90.3 2.1 collective-permute-start
  92.4 7.9 %collective-permute-start.1 = (bf16[128,1024]{1,0:T(8,128)(2,1)S(1)}, bf16[128,1024]{1,0:T(8,128)(2,1)}, u32[]{:S(2)}, u32[]{:S(2)}) collective-permute-start(bf16[128,1024]{1,0:T(8,128)(2,1)S(1)} %pad_maximum_fusion.1), channel_id=1, source_target_pairs={{1,0},{2,1},{3,2},{4,3},{5,4},{6,5},{7,6},{8,7},{9,8},{10,9},{11,1... | collective-permute-start | bytes 786440 | tf_op jit(solution)/shard_map/ppermute | solution.py:20
  100.3 55.4 %all-reduce.3.cloned.1.call-done = f32[8,128,128]{2,1,0:T(8,128)} async-done(((f32[8,128,128]{2,1,0:T(8,128)}), f32[8,128,128]{2,1,0:T(8,128)}) %all-reduce.3.cloned.1.call-update) | async-done | bytes 524304 | tf_op jit(solution)/shard_map/psum | solution.py:53
  155.8 13.3 %psum.30 = f32[8,128]{1,0:T(8,128)S(1)} all-reduce(f32[8,128]{1,0:T(8,128)S(1)} %fusion.16), channel_id=1, replica_groups=mesh['ctxa'=32,'ctxb'=8] {'ctxb'}, use_global_device_ids=true, to_apply=%region_9.0 | all-reduce | flops 1024 | bytes 8192 | tf_op jit(solution)/shard_map/psum | solution.py:53
  169.1 63.2 %psum.31 = f32[8,128]{1,0:T(8,128)S(1)} all-reduce(f32[8,128]{1,0:T(8,128)S(1)} %psum.30), channel_id=1, replica_groups=mesh['ctxa'=32,'ctxb'=8] {'ctxa'}, use_global_device_ids=true, to_apply=%region_10.0 | all-reduce | flops 1024 | bytes 8192 | tf_op jit(solution)/shard_map/psum | solution.py:53
  232.3 0.3 convolution_convert_fusion.1
  232.7 1.1 pad_maximum_fusion
  233.8 0.4 copy.24
  234.1 71.7 %all-reduce.5.cloned.1.call-done = f32[8,128,128]{2,1,0:T(8,128)} async-done(((f32[8,128,128]{2,1,0:T(8,128)}), f32[8,128,128]{2,1,0:T(8,128)}) %all-reduce.5.cloned.1.call-update) | async-done | bytes 524304 | tf_op jit(solution)/shard_map/psum | solution.py:53
  305.9 1.3 slice_reduce_fusion
  307.2 1.4 multiply_reduce_fusion
  308.6 0.6 fusion.15
  309.5 12.2 %while.12 = (s32[]{:T(128)}, bf16[2,128,256]{1,2,0:T(8,128)(2,1)}, s32[2]{0:T(128)S(1)}, bf16[384,1024]{0,1:T(8,128)(2,1)S(1)}, s32[]{:T(128)}, /*index=5*/bf16[...) while((s32[]{:T(128)}, bf16[2,128,256]{1,2,0:T(8,128)(2,1)}, ...), condition=%wide.region_16.17_spmd, body=%wide.region_11.16_spmd.sunk | while | flops 69452448 | bytes 5446203 | solution.py:118
  309.6 0.7 dynamic_slice.60
  313.4 0.4 fusion.63
  313.8 0.3 fusion.60
  314.1 0.3 fusion.64
  314.6 0.4 fusion.67
  315.0 0.6 constant_dynamic-update-slice_fusion.2
  315.7 0.7 dynamic_slice.60
  319.5 0.4 fusion.63
  319.9 0.3 fusion.60
  320.2 0.3 fusion.64
  320.7 0.4 fusion.67
  321.1 0.6 constant_dynamic-update-slice_fusion.2
  321.8 1.9 convolution_convert_fusion
  (60 shorter events, 2.5 us)
Async XLA Ops:
  6.5 315.2 %copy-start = (bf16[512,1024]{1,0:T(8,128)(2,1)S(1)}, bf16[512,1024]{1,0:T(8,128)(2,1)}, u32[]{:S(2)}) copy-start(bf16[512,1024]{1,0:T(8,128)(2,1)} %param.13) | copy-start | bytes 3145732
  6.5 2.1 copy-start.5
  6.5 149.1 %all-reduce.3.cloned.1.call-start = ((), (), s32[]{:S(2)}) async-start(), calls=%async_computation | async-start | bytes 1048576 | tf_op jit(solution)/shard_map/psum | solution.py:53
  8.3 79.3 %copy-start.2 = (bf16[128,1024]{1,0:T(8,128)(2,1)S(1)}, bf16[128,1024]{1,0:T(8,128)(2,1)}, u32[]{:S(2)}) copy-start(bf16[128,1024]{1,0:T(8,128)(2,1)} %param.8) | copy-start | bytes 786436
  8.3 79.3 %copy-start.3 = (bf16[1024,512]{1,0:T(8,128)(2,1)S(1)}, bf16[1024,512]{1,0:T(8,128)(2,1)}, u32[]{:S(2)}) copy-start(bf16[1024,512]{1,0:T(8,128)(2,1)} %param.11) | copy-start | bytes 3145732
  89.8 216.1 %all-reduce.5.cloned.1.call-start = ((), (), s32[]{:S(2)}) async-start(), calls=%async_computation.1 | async-start | bytes 1048576 | tf_op jit(solution)/shard_map/psum | solution.py:53
  90.3 142.0 %copy-start.4 = (bf16[1024,512]{1,0:T(8,128)(2,1)S(1)}, bf16[1024,512]{1,0:T(8,128)(2,1)}, u32[]{:S(2)}) copy-start(bf16[1024,512]{1,0:T(8,128)(2,1)} %param.9) | copy-start | bytes 3145732
  90.3 142.3 %collective-permute-start = (bf16[128,1024]{1,0:T(8,128)(2,1)S(1)}, bf16[128,1024]{1,0:T(8,128)(2,1)}, u32[]{:S(2)}, u32[]{:S(2)}) collective-permute-start(bf16[128,1024]{1,0:T(8,128)(2,1)S(1)} %pad_maximum_fusion.1), channel_id=1, source_target_pairs={{0,1},{1,2},{2,3},{3,4},{4,5},{5,6},{6,7},{7,8},{8,9},{9,10},{10,1... | collective-permute-start | bytes 786440 | tf_op jit(solution)/shard_map/ppermute | solution.py:17
  92.4 140.2 %collective-permute-start.1 = (bf16[128,1024]{1,0:T(8,128)(2,1)S(1)}, bf16[128,1024]{1,0:T(8,128)(2,1)}, u32[]{:S(2)}, u32[]{:S(2)}) collective-permute-start(bf16[128,1024]{1,0:T(8,128)(2,1)S(1)} %pad_maximum_fusion.1), channel_id=1, source_target_pairs={{1,0},{2,1},{3,2},{4,3},{5,4},{6,5},{7,6},{8,7},{9,8},{10,9},{11,1... | collective-permute-start | bytes 786440 | tf_op jit(solution)/shard_map/ppermute | solution.py:20
  305.9 2.8 copy-start.1
Sparse Core Ops, SparseCore 0:
  89.9 65.7 all-reduce.2
  159.1 146.7 all-reduce.4
